TPU v7x, 32 devices: a whole 2x2x4 slice. The times are simulated.
32 devices in a mesh: tx: 4 (over y, x), ty: 2 (over core), depth: 4 (over z).
Axes of the slice: x: 2, y: 2, z: 4, core: 2. Of those that a mesh axis runs over, the one named last changes fastest.
Arguments:
- volume: bfloat16 [128, 512, 512], P('depth', 'ty', 'tx'), may hold values from -6 to 6
- transfer: float32 [4, 2], replicated, may hold values from -1.5 to 1.5
- ray_start: int32 [4, 512, 512], P('depth', 'ty', 'tx'), may hold values from 0 to 15
- ray_stop: int32 [4, 512, 512], P('depth', 'ty', 'tx'), may hold values from 16 to 32
- pattern: int32 [4, 64, 4], P('depth', 'ty', 'tx'), may hold values 0 or 1
- depth_order: int32 [4], replicated, may hold values from 0 to 3, each once
Outputs:
- frame: float32 [4, 512, 512], P(None, 'ty', 'tx')
Inputs may be any that keep to these rules, and one draw needn't show every extreme that they name: ray_start[s] < ray_stop[s] for every ray and slice. `depth_order`: each slice appears once.
All inputs are finite; a program needn't handle non-finite values. No bound on the sum of `pattern` on one device may be relied on, other than what follows from the above.
Results may differ from a plain program's by a relative error of at most 0.0003.
Values may be sent and summed in bfloat16 or wider, within the bound.
A program may use at most 64 MiB of HBM per device.

v0:
```python
import jax
import jax.numpy as jnp
from jax import lax
from jax.sharding import PartitionSpec as P


def with_halo(array, sides, width):
    for axis, dim in sides:
        count, length = (lax.axis_size(axis), array.shape[dim])
        up = [(i, (i + 1) % count) for i in range(count - 1)]
        down = [(j, i) for i, j in up]
        last = lax.slice_in_dim(array, length - width, length, axis=dim)
        initial = lax.slice_in_dim(array, 0, width, axis=dim)
        before = lax.ppermute(last, axis, up)
        after = lax.ppermute(initial, axis, down)
        array = jnp.concatenate([before, array, after], axis=dim)
    return array


def local_partial(padded, transfer, ray_start, ray_stop, pattern, depth_count):
    samples = padded.shape[0] - 2
    values = padded[1:-1, 1:-1, 1:-1]
    grad_z = (padded[2:, 1:-1, 1:-1] - padded[:-2, 1:-1, 1:-1]) * 0.5
    grad_y = (padded[1:-1, 2:, 1:-1] - padded[1:-1, :-2, 1:-1]) * 0.5
    grad_x = (padded[1:-1, 1:-1, 2:] - padded[1:-1, 1:-1, :-2]) * 0.5
    lit = jnp.abs(0.48 * grad_x + 0.6 * grad_y + 0.64 * grad_z)
    shading = 0.3 + 0.7 * lit / jnp.sqrt(grad_x * grad_x + grad_y * grad_y + grad_z * grad_z + 1.0)
    rows_each = ray_start.shape[0] // pattern.shape[0]
    cols_each = ray_start.shape[1] // pattern.shape[1]
    pattern_full = jnp.repeat(jnp.repeat(pattern, rows_each, axis=0), cols_each, axis=1)
    layers = lax.broadcasted_iota(jnp.int32, (samples, 1, 1), 0)
    active = (layers >= ray_start[None]) & (layers < ray_stop[None]) & (pattern_full[None] > 0)
    density = jax.nn.softplus(transfer[3, 0] * values + transfer[3, 1]) * (
        2.0 / (samples * depth_count)
    )
    opacity = jnp.where(active, 1.0 - jnp.exp(-density), jnp.float32(0.0))
    passed = jnp.cumprod(1.0 - opacity, axis=0)
    prior = jnp.concatenate([jnp.ones_like(passed[:1]), passed[:-1]], axis=0)
    weights = prior * opacity * shading
    tinted = jax.nn.sigmoid(
        transfer[:3, 0][:, None, None, None] * values[None] + transfer[:3, 1][:, None, None, None]
    )
    colors = jnp.sum(weights[None] * tinted, axis=1)
    return jnp.concatenate([colors, passed[-1][None]], axis=0)


def composite(partials, depth_order):
    count = partials.shape[0]

    def step(position, state_pair):
        colors, remain = state_pair
        slice_part = lax.dynamic_index_in_dim(partials, depth_order[position], 0, keepdims=False)
        return (colors + remain[None] * slice_part[:3], remain * slice_part[3])

    start_pair = (
        jnp.zeros((3,) + partials.shape[2:], jnp.float32),
        jnp.ones(partials.shape[2:], jnp.float32),
    )
    colors, remain = lax.fori_loop(0, count, step, start_pair)
    return jnp.concatenate([colors, 1.0 - remain[None]], axis=0)


def shards(volume, transfer, ray_start, ray_stop, pattern, depth_order):
    padded = with_halo(volume, (("tx", 2), ("ty", 1), ("depth", 0)), 1).astype(jnp.float32)
    depth_count = lax.axis_size("depth")
    stacked = local_partial(padded, transfer, ray_start[0], ray_stop[0], pattern[0], depth_count)[
        None
    ]
    pixel_share = lax.all_to_all(stacked, "depth", split_axis=2, concat_axis=0, tiled=True)
    picture = composite(pixel_share, depth_order)
    return lax.all_gather(picture, "depth", axis=1, tiled=True)


def solution(mesh):
    in_specs = (
        P("depth", "ty", "tx"),
        P(),
        P("depth", "ty", "tx"),
        P("depth", "ty", "tx"),
        P("depth", "ty", "tx"),
        P(),
    )
    out_specs = P(None, "ty", "tx")
    return jax.shard_map(shards, mesh=mesh, in_specs=in_specs, out_specs=out_specs, check_vma=False)
```

profile of v0, /device:TPU:0, one launch (start us, length us, event | category | flops | bytes accessed | tf_op | source)
XLA Modules:
  0.0 122.1 jit_solution(3508607483782264518)
XLA Ops:
  0.0 5.0 %fusion.15 = (bf16[32,256,1]{2,1,0:T(8,128)(2,1)}, bf16[32,256,1]{2,1,0:T(8,128)(2,1)}) fusion(bf16[32,256,128]{2,1,0:T(8,128)(2,1)} %param.8), kind=kLoop, calls=%fused_computation.41 | loop fusion | bytes 65536 | tf_op jit(solution)/shard_map/slice | solution.py:12
  5.0 2.1 %copy.24 = bf16[32,256,1]{1,0,2:T(8,128)(2,1)S(1)} copy(bf16[32,256,1]{2,1,0:T(8,128)(2,1)} %get-tuple-element.154) | data formatting | bytes 32768
  7.1 1.3 %collective-permute-start.1 = (bf16[32,256,1]{1,0,2:T(8,128)(2,1)S(1)}, bf16[32,256,1]{1,0,2:T(8,128)(2,1)S(1)}, u32[]{:S(2)}, u32[]{:S(2)}) collective-permute-start(bf16[32,256,1]{1,0,2:T(8,128)(2,1)S(1)} %copy.24), channel_id=1, source_target_pairs={{8,0},{16,8},{24,16},{9,1},{17,9},{25,17},{10,2},{18,10},{26,18},{... | collective-permute-start | bytes 49160 | tf_op jit(solution)/shard_map/ppermute | solution.py:15
  8.4 2.0 %copy.23 = bf16[32,256,1]{1,0,2:T(8,128)(2,1)S(1)} copy(bf16[32,256,1]{2,1,0:T(8,128)(2,1)} %get-tuple-element.153) | data formatting | bytes 32768
  10.4 5.5 %collective-permute-start = (bf16[32,256,1]{1,0,2:T(8,128)(2,1)S(1)}, bf16[32,256,1]{1,0,2:T(8,128)(2,1)S(1)}, u32[]{:S(2)}, u32[]{:S(2)}) collective-permute-start(bf16[32,256,1]{1,0,2:T(8,128)(2,1)S(1)} %copy.23), channel_id=1, source_target_pairs={{0,8},{8,16},{16,24},{1,9},{9,17},{17,25},{2,10},{10,18},{18,26},{... | collective-permute-start | bytes 49160 | tf_op jit(solution)/shard_map/ppermute | solution.py:14
  15.9 0.0 copy-done.6
  15.9 1.4 %collective-permute-done = bf16[32,256,1]{1,0,2:T(8,128)(2,1)S(1)} collective-permute-done((bf16[32,256,1]{1,0,2:T(8,128)(2,1)S(1)}, bf16[32,256,1]{1,0,2:T(8,128)(2,1)S(1)}, u32[]{:S(2)}, u32[]{:S(2)}) %collective-permute-start) | collective-permute-done | bytes 16416 | tf_op jit(solution)/shard_map/ppermute | solution.py:14
  17.3 1.8 %copy.17 = bf16[32,256,1]{2,1,0:T(8,128)(2,1)} copy(bf16[32,256,1]{1,0,2:T(8,128)(2,1)S(1)} %collective-permute-done) | data formatting | bytes 32768 | tf_op jit(solution)/shard_map/ppermute | solution.py:14
  19.1 0.0 collective-permute-done.1
  19.1 1.8 %copy.18 = bf16[32,256,1]{2,1,0:T(8,128)(2,1)} copy(bf16[32,256,1]{1,0,2:T(8,128)(2,1)S(1)} %collective-permute-done.1) | data formatting | bytes 32768 | tf_op jit(solution)/shard_map/ppermute | solution.py:15
  21.0 0.0 copy-done
  21.0 1.2 pad_maximum_fusion.8
  22.1 1.3 %collective-permute-start.2 = (bf16[32,1,130]{2,1,0:T(2,128)(2,1)S(1)}, bf16[32,1,130]{2,1,0:T(2,128)(2,1)S(1)}, u32[]{:S(2)}, u32[]{:S(2)}) collective-permute-start(bf16[32,1,130]{2,1,0:T(2,128)(2,1)S(1)} %get-tuple-element.151), channel_id=1, source_target_pairs={{0,4},{1,5},{2,6},{3,7},{8,12},{9,13},{10,14},{11,15},{16,20},{17,... | collective-permute-start | bytes 24968 | tf_op jit(solution)/shard_map/ppermute | solution.py:14
  23.4 1.3 %collective-permute-start.3 = (bf16[32,1,130]{2,1,0:T(2,128)(2,1)S(1)}, bf16[32,1,130]{2,1,0:T(2,128)(2,1)S(1)}, u32[]{:S(2)}, u32[]{:S(2)}) collective-permute-start(bf16[32,1,130]{2,1,0:T(2,128)(2,1)S(1)} %get-tuple-element.152), channel_id=1, source_target_pairs={{4,0},{5,1},{6,2},{7,3},{12,8},{13,9},{14,10},{15,11},{20,16},{21,... | collective-permute-start | bytes 24968 | tf_op jit(solution)/shard_map/ppermute | solution.py:15
  24.7 0.0 copy-done.7
  24.7 0.1 broadcast_in_dim.24
  24.8 0.1 gt.22
  24.9 0.0 copy-start.1
  24.9 0.0 copy-start.2
  24.9 0.0 copy-start.3
  24.9 0.0 collective-permute-done.2
  25.0 1.6 %collective-permute-done.3 = bf16[32,1,130]{2,1,0:T(2,128)(2,1)S(1)} collective-permute-done((bf16[32,1,130]{2,1,0:T(2,128)(2,1)S(1)}, bf16[32,1,130]{2,1,0:T(2,128)(2,1)S(1)}, u32[]{:S(2)}, u32[]{:S(2)}) %collective-permute-start.3) | collective-permute-done | bytes 8352 | tf_op jit(solution)/shard_map/ppermute | solution.py:15
  26.5 1.4 %pad_maximum_fusion.4 = (bf16[1,258,130]{2,1,0:T(8,128)(2,1)S(1)}, bf16[1,258,130]{2,1,0:T(8,128)(2,1)S(1)}) fusion(bf16[32,1,130]{2,1,0:T(2,128)(2,1)S(1)} %collective-permute-done.3, bf16[32,1,130]{2,1,0:T(2,128)(2,1)S(1)} %collective-permute-done.2, bf16[32,256,1]{2,1,0:T(8,128)(2,1)} %copy.18, bf16[32,256,128]{2,1,0:T(8,128)(2,1)S(1)} %copy-done, ...), kind=kLoop, calls=%fused_computation.31 | loop fusion | flops 670800 | bytes 2280720 | tf_op jit(solution)/shard_map/slice | solution.py:12
  28.0 4.0 %collective-permute-start.4 = (bf16[1,258,130]{2,1,0:T(8,128)(2,1)S(1)}, bf16[1,258,130]{2,1,0:T(8,128)(2,1)S(1)}, u32[]{:S(2)}, u32[]{:S(2)}) collective-permute-start(bf16[1,258,130]{2,1,0:T(8,128)(2,1)S(1)} %get-tuple-element.149), channel_id=1, source_target_pairs={{0,1},{1,2},{2,3},{4,5},{5,6},{6,7},{8,9},{9,10},{10,11},{12,13},{... | collective-permute-start | bytes 201248 | tf_op jit(solution)/shard_map/ppermute | solution.py:14
  32.0 1.5 %collective-permute-start.5 = (bf16[1,258,130]{2,1,0:T(8,128)(2,1)S(1)}, bf16[1,258,130]{2,1,0:T(8,128)(2,1)S(1)}, u32[]{:S(2)}, u32[]{:S(2)}) collective-permute-start(bf16[1,258,130]{2,1,0:T(8,128)(2,1)S(1)} %get-tuple-element.150), channel_id=1, source_target_pairs={{1,0},{2,1},{3,2},{5,4},{6,5},{7,6},{9,8},{10,9},{11,10},{13,12},{... | collective-permute-start | bytes 201248 | tf_op jit(solution)/shard_map/ppermute | solution.py:15
  33.4 0.6 fusion.16
  34.1 1.1 collective-permute-done.4
  35.2 4.1 %collective-permute-done.5 = bf16[1,258,130]{2,1,0:T(8,128)(2,1)S(1)} collective-permute-done((bf16[1,258,130]{2,1,0:T(8,128)(2,1)S(1)}, bf16[1,258,130]{2,1,0:T(8,128)(2,1)S(1)}, u32[]{:S(2)}, u32[]{:S(2)}) %collective-permute-start.5) | collective-permute-done | bytes 67112 | tf_op jit(solution)/shard_map/ppermute | solution.py:15
  39.3 0.0 copy-done.1
  39.3 0.0 copy-done.2
  39.3 0.0 copy-done.3
  39.3 7.2 %maximum_convert_fusion = f32[34,258,130]{2,1,0:T(8,128)S(1)} fusion(bf16[1,258,130]{2,1,0:T(8,128)(2,1)S(1)} %collective-permute-done.5, bf16[32,1,130]{2,1,0:T(2,128)(2,1)S(1)} %collective-permute-done.3, bf16[32,256,1]{2,1,0:T(8,128)(2,1)S(1)} %copy-done.3, bf16[32,256,128]{2,1,0:T(8,128)(2,1)S(1)} %copy-done.1, bf16[32,256,1]{2,1,0:T(8,128)(2,1)S(1)} %copy-done.2, ...), kind=kLoop, calls=%fused_computation.9 | loop fusion | flops 15965040 | bytes 6842160 | tf_op jit(solution)/shard_map/convert_element_type | solution.py:64
  46.5 7.6 %fusion.8 = f32[32,256,128]{2,1,0:T(8,128)} fusion(f32[]{:T(128)} %bitcast.4, f32[]{:T(128)} %bitcast.3, s32[256,128]{1,0:T(8,128)S(1)} %bitcast.41, s32[256,128]{1,0:T(8,128)S(1)} %bitcast.43, pred[256]{0:T(512)(128)(4,1)S(1)} %gt.22, f32[34,258,130]{2,1,0:T(8,128)S(1)} %maximum_convert_fusion), kind=kOutput, calls=%fused_computation.19 | output fusion | flops 50331648 | bytes 8651272 | tf_op jit(solution)/shard_map/jit(cumprod)/reduce_window | solution.py:37
  54.1 4.5 %slice.100 = f32[31,256,128]{2,1,0:T(8,128)} slice(f32[32,256,128]{2,1,0:T(8,128)} %fusion.8), slice={[0:31], [0:256], [0:128]} | slice | bytes 8126464 | tf_op jit(solution)/shard_map/slice | solution.py:38
  58.6 13.5 %add_multiply_fusion = (f32[32,256,128]{2,1,0:T(8,128)S(1)}, f32[32,256,128]{2,1,0:T(8,128)S(1)}) fusion(f32[34,258,130]{2,1,0:T(8,128)S(1)} %maximum_convert_fusion, f32[31,256,128]{2,1,0:T(8,128)} %slice.100, f32[]{:T(128)} %bitcast.4, f32[]{:T(128)} %bitcast.3, pred[256]{0:T(512)(128)(4,1)S(1)} %gt.22, s32[256,128]{1,0:T(8,128)S(1)} %bitcast.42, ...), kind=kLoop, calls=%fused_computation.18 | loop fusion | flops 40894464 | bytes 42074376 | tf_op jit(solution)/shard_map/mul | solution.py:39
  72.1 0.0 slice-start
  72.1 3.8 %multiply_reduce_fusion = f32[3,256,128]{2,1,0:T(8,128)S(1)} fusion(f32[3]{0:T(128)S(1)} %get-tuple-element.156, f32[32,256,128]{2,1,0:T(8,128)S(1)} %get-tuple-element.148, f32[3]{0:T(128)S(1)} %get-tuple-element.155, f32[32,256,128]{2,1,0:T(8,128)S(1)} %get-tuple-element.147), kind=kLoop, calls=%fused_computation.7 | loop fusion | flops 21921792 | bytes 8781848 | tf_op jit(solution)/shard_map/reduce_sum | solution.py:43
  76.0 0.0 copy-start.8
  76.0 1.1 copy.19
  77.2 3.9 %all-to-all-start = ((f32[1,4,256,128]{3,1,0,2:T(4,128)}), f32[1,4,256,128]{3,1,0,2:T(4,128)S(1)}, u32[]{:S(2)}, u32[]{:S(2)}) async-start(f32[1,4,256,128]{3,1,0,2:T(4,128)} %copy.19), calls=%async_computation | async-start | bytes 1048576 | tf_op jit(solution)/shard_map/all_to_all | solution.py:69
  81.0 13.7 %all-to-all-done = f32[1,4,256,128]{3,1,0,2:T(4,128)S(1)} async-done(((f32[1,4,256,128]{3,1,0,2:T(4,128)}), f32[1,4,256,128]{3,1,0,2:T(4,128)S(1)}, u32[]{:S(2)}, u32[]{:S(2)}) %all-to-all-start) | async-done | bytes 524320 | tf_op jit(solution)/shard_map/all_to_all | solution.py:69
  94.8 10.5 %while.16 = (s32[]{:T(128)}, f32[3,64,128]{2,1,0:T(8,128)S(1)}, f32[64,128]{1,0:T(8,128)S(1)}, s32[4]{0:T(128)S(1)}, f32[4,4,64,128]{3,2,0,1:T(8,128)S(1)}, /*index=5*/s32[]{:T(128)}, s32[]{:T(128)}, s32[]{:T(128)}) while((s32[]{:T(128)}, f32[3,64,128]{2,1,0:T(8,128)S(1)}, f32[64,128]{1,0:T(8,128)S(1)}, s32[4]{0:T(128)S(1)}, ...), condition=%wide.region_3.4_spmd.clone, body=%wide.region_2.3_spmd.clone.sunk | while | flops 90118 | bytes 721050 | solution.py:59
  94.8 0.6 dynamic_slice.21
  97.5 0.6 dynamic_slice.21
  100.1 0.6 dynamic_slice.21
  102.7 0.6 dynamic_slice.21
  105.4 15.9 %all_gather.3 = f32[4,256,128]{2,1,0:T(8,128)S(1)} all-gather(f32[4,64,128]{2,1,0:T(8,128)S(1)} %pad_maximum_fusion.5), channel_id=1, replica_groups=mesh['tx'=4,'ty'=2,'depth'=4] {'depth'}, dimensions={1}, use_global_device_ids=true | all-gather | bytes 655360 | tf_op jit(solution)/shard_map/all_gather | solution.py:71
  121.3 0.8 copy.35
  (29 shorter events, 0.3 us)
Async XLA Ops:
  5.0 10.9 %copy-start.6 = (f32[4,2]{0,1:T(2,128)S(1)}, f32[4,2]{0,1:T(2,128)}, u32[]{:S(2)}) copy-start(f32[4,2]{0,1:T(2,128)} %param.9) | copy-start | bytes 100
  5.0 16.0 %copy-start = (bf16[32,256,128]{2,1,0:T(8,128)(2,1)S(1)}, bf16[32,256,128]{2,1,0:T(8,128)(2,1)}, u32[]{:S(2)}) copy-start(bf16[32,256,128]{2,1,0:T(8,128)(2,1)} %param.8) | copy-start | bytes 6291460
  7.1 12.0 %collective-permute-start.1 = (bf16[32,256,1]{1,0,2:T(8,128)(2,1)S(1)}, bf16[32,256,1]{1,0,2:T(8,128)(2,1)S(1)}, u32[]{:S(2)}, u32[]{:S(2)}) collective-permute-start(bf16[32,256,1]{1,0,2:T(8,128)(2,1)S(1)} %copy.24), channel_id=1, source_target_pairs={{8,0},{16,8},{24,16},{9,1},{17,9},{25,17},{10,2},{18,10},{26,18},{... | collective-permute-start | bytes 49160 | tf_op jit(solution)/shard_map/ppermute | solution.py:15
  10.4 6.9 %collective-permute-start = (bf16[32,256,1]{1,0,2:T(8,128)(2,1)S(1)}, bf16[32,256,1]{1,0,2:T(8,128)(2,1)S(1)}, u32[]{:S(2)}, u32[]{:S(2)}) collective-permute-start(bf16[32,256,1]{1,0,2:T(8,128)(2,1)S(1)} %copy.23), channel_id=1, source_target_pairs={{0,8},{8,16},{16,24},{1,9},{9,17},{17,25},{2,10},{10,18},{18,26},{... | collective-permute-start | bytes 49160 | tf_op jit(solution)/shard_map/ppermute | solution.py:14
  19.1 5.6 %copy-start.7 = (s32[1,32,1]{1,2,0:T(1,128)S(1)}, s32[1,32,1]{1,2,0:T(1,128)}, u32[]{:S(2)}) copy-start(s32[1,32,1]{1,2,0:T(1,128)} %param.12) | copy-start | bytes 388
  22.1 2.8 %collective-permute-start.2 = (bf16[32,1,130]{2,1,0:T(2,128)(2,1)S(1)}, bf16[32,1,130]{2,1,0:T(2,128)(2,1)S(1)}, u32[]{:S(2)}, u32[]{:S(2)}) collective-permute-start(bf16[32,1,130]{2,1,0:T(2,128)(2,1)S(1)} %get-tuple-element.151), channel_id=1, source_target_pairs={{0,4},{1,5},{2,6},{3,7},{8,12},{9,13},{10,14},{11,15},{16,20},{17,... | collective-permute-start | bytes 24968 | tf_op jit(solution)/shard_map/ppermute | solution.py:14
  23.4 3.1 %collective-permute-start.3 = (bf16[32,1,130]{2,1,0:T(2,128)(2,1)S(1)}, bf16[32,1,130]{2,1,0:T(2,128)(2,1)S(1)}, u32[]{:S(2)}, u32[]{:S(2)}) collective-permute-start(bf16[32,1,130]{2,1,0:T(2,128)(2,1)S(1)} %get-tuple-element.152), channel_id=1, source_target_pairs={{4,0},{5,1},{6,2},{7,3},{12,8},{13,9},{14,10},{15,11},{20,16},{21,... | collective-permute-start | bytes 24968 | tf_op jit(solution)/shard_map/ppermute | solution.py:15
  24.9 14.4 %copy-start.1 = (bf16[32,256,128]{2,1,0:T(8,128)(2,1)S(1)}, bf16[32,256,128]{2,1,0:T(8,128)(2,1)}, u32[]{:S(2)}) copy-start(bf16[32,256,128]{2,1,0:T(8,128)(2,1)} %param.8) | copy-start | bytes 6291460
  24.9 14.4 %copy-start.2 = (bf16[32,256,1]{2,1,0:T(8,128)(2,1)S(1)}, bf16[32,256,1]{2,1,0:T(8,128)(2,1)}, u32[]{:S(2)}) copy-start(bf16[32,256,1]{2,1,0:T(8,128)(2,1)} %copy.17) | copy-start | bytes 49156
  24.9 14.4 %copy-start.3 = (bf16[32,256,1]{2,1,0:T(8,128)(2,1)S(1)}, bf16[32,256,1]{2,1,0:T(8,128)(2,1)}, u32[]{:S(2)}) copy-start(bf16[32,256,1]{2,1,0:T(8,128)(2,1)} %copy.18) | copy-start | bytes 49156
  28.0 7.2 %collective-permute-start.4 = (bf16[1,258,130]{2,1,0:T(8,128)(2,1)S(1)}, bf16[1,258,130]{2,1,0:T(8,128)(2,1)S(1)}, u32[]{:S(2)}, u32[]{:S(2)}) collective-permute-start(bf16[1,258,130]{2,1,0:T(8,128)(2,1)S(1)} %get-tuple-element.149), channel_id=1, source_target_pairs={{0,1},{1,2},{2,3},{4,5},{5,6},{6,7},{8,9},{9,10},{10,11},{12,13},{... | collective-permute-start | bytes 201248 | tf_op jit(solution)/shard_map/ppermute | solution.py:14
  32.0 7.3 %collective-permute-start.5 = (bf16[1,258,130]{2,1,0:T(8,128)(2,1)S(1)}, bf16[1,258,130]{2,1,0:T(8,128)(2,1)S(1)}, u32[]{:S(2)}, u32[]{:S(2)}) collective-permute-start(bf16[1,258,130]{2,1,0:T(8,128)(2,1)S(1)} %get-tuple-element.150), channel_id=1, source_target_pairs={{1,0},{2,1},{3,2},{5,4},{6,5},{7,6},{9,8},{10,9},{11,10},{13,12},{... | collective-permute-start | bytes 201248 | tf_op jit(solution)/shard_map/ppermute | solution.py:15
  34.1 12.4 %copy-start.4 = (s32[1,256,128]{2,1,0:T(8,128)S(1)}, s32[1,256,128]{2,1,0:T(8,128)}, u32[]{:S(2)}) copy-start(s32[1,256,128]{2,1,0:T(8,128)} %param.11) | copy-start | bytes 393220
  34.1 12.4 %copy-start.5 = (s32[1,256,128]{2,1,0:T(8,128)S(1)}, s32[1,256,128]{2,1,0:T(8,128)}, u32[]{:S(2)}) copy-start(s32[1,256,128]{2,1,0:T(8,128)} %param.10) | copy-start | bytes 393220
  72.1 3.8 %slice-start = ((f32[32,256,128]{2,1,0:T(8,128)}), f32[1,256,128]{2,1,0:T(8,128)S(1)}, s32[]{:S(2)}) async-start(f32[32,256,128]{2,1,0:T(8,128)} %fusion.8), calls=%async_computation.1 | async-start | bytes 262144 | tf_op jit(solution)/shard_map/slice | solution.py:44
  76.0 18.8 %copy-start.8 = (s32[4]{0:T(128)S(1)}, s32[4]{0:T(128)}, u32[]{:S(2)}) copy-start(s32[4]{0:T(128)} %param.13) | copy-start | bytes 52
  77.2 17.6 %all-to-all-start = ((f32[1,4,256,128]{3,1,0,2:T(4,128)}), f32[1,4,256,128]{3,1,0,2:T(4,128)S(1)}, u32[]{:S(2)}, u32[]{:S(2)}) async-start(f32[1,4,256,128]{3,1,0,2:T(4,128)} %copy.19), calls=%async_computation | async-start | bytes 1048576 | tf_op jit(solution)/shard_map/all_to_all | solution.py:69
where the time goes:
time: 124 us; the launch traced here: 122 us
  other arithmetic  34.9 us (28%)
  local copies, waits for them, and re-layouts  22.5 us (18%)
  waiting for transfers between devices  21.9 us (18%)
  starting transfers between devices  18.7 us (15%)
  blocking collectives  15.9 us (13%)
  loops' own time  7.94 us (6%)
    all_gather x1, blocking collectives, shards(): return lax.all_gather(picture, 'depth', axis=1, tiled=True)  15.9 us
    all_to_all x1, waiting for transfers between devices, shards(): lax.all_to_all(stacked, 'depth', split_axis=2, concat_axis=0, tiled=True)  13.7 us
    mul x1, other arithmetic, local_partial(): weights = prior * opacity * shading  13.5 us
    ppermute x3, starting transfers between devices, with_halo(): before = lax.ppermute(last, axis, up)  10.8 us
    another operation x1, loops' own time, composite(): colors, remain = lax.fori_loop(0, count, step, start_pair)  7.94 us
    another operation x1, other arithmetic, local_partial(): passed = jnp.cumprod(1.0 - opacity, axis=0)  7.56 us
    convert_element_type x1, other arithmetic, shards(): with_halo(volume, (('tx', 2), ('ty', 1), ('depth', 0)), 1)  7.22 us
    ppermute x3, waiting for transfers between devices, with_halo(): after = lax.ppermute(initial, axis, down)  5.69 us
  transfers between devices with their start and end apart: 7, of which 5 were waited for; matrix products, arithmetic and copies ran while one was open for 4% of the time, Pallas kernels for 0%

commit v1 on v0

v1 whole, which is shorter than its diff:
```python
import functools
import math

import jax
import jax.numpy as jnp
from jax import lax
from jax.experimental import pallas as pl
from jax.experimental.pallas import tpu as pltpu
from jax.sharding import PartitionSpec as P

MESH = pl.DeviceIdType.MESH
ROWS = 16
LAG = 5
UNROLL = 8
LOG2E = math.log2(math.e)


def band(length, across):
    r = lax.broadcasted_iota(jnp.int32, (length, length), 0)
    c = lax.broadcasted_iota(jnp.int32, (length, length), 1)
    up, down = (r == c + 1, r + 1 == c) if across else (c == r + 1, c + 1 == r)
    return (up.astype(jnp.float32) - down.astype(jnp.float32)).astype(jnp.bfloat16)


def dot(a, b):
    return jnp.dot(a, b, preferred_element_type=jnp.float32)


def kernel(
    n, n_tx, n_ty, scale,
    vol, start_hbm, stop_hbm, pattern, transfer, order, out,
    vb, start, stop, yup, ydn, edge, xl, xr, gx, gy, dy, part, parts, fin,
    load_sem, halo_send, halo_recv, part_send, part_recv, fin_send, fin_recv,
):
    samples, ny, nx = vol.shape
    half = ny // 2
    chunks = ny // ROWS
    owned = chunks // n
    tx, ty, me = lax.axis_index("tx"), lax.axis_index("ty"), lax.axis_index("depth")

    loads = [
        pltpu.make_async_copy(vol, vb.at[pl.ds(1, samples)], load_sem.at[0]),
        pltpu.make_async_copy(start_hbm.at[0], start, load_sem.at[1]),
        pltpu.make_async_copy(stop_hbm.at[0], stop, load_sem.at[2]),
    ]
    for load in loads:
        load.start()

    barrier = pltpu.get_barrier_semaphore()
    for rel in range(1, n):
        pl.semaphore_signal(barrier, inc=1, device_id={"depth": lax.rem(me + rel, n)}, device_id_type=MESH)
    sides = (("tx", tx, n_tx), ("ty", ty, n_ty))
    expected = n - 1
    for axis, at, count in sides:
        @pl.when(at > 0)
        def _(axis=axis, at=at):
            pl.semaphore_signal(barrier, inc=1, device_id={axis: at - 1}, device_id_type=MESH)

        @pl.when(at < count - 1)
        def _(axis=axis, at=at):
            pl.semaphore_signal(barrier, inc=1, device_id={axis: at + 1}, device_id_type=MESH)

        expected = expected + jnp.where(at > 0, 1, 0) + jnp.where(at < count - 1, 1, 0)
    pl.semaphore_wait(barrier, expected)

    def shift(slot, axis, at, count, source, target, upward):
        return pltpu.make_async_remote_copy(
            src_ref=source, dst_ref=target, send_sem=halo_send.at[slot], recv_sem=halo_recv.at[slot],
            device_id={axis: at + 1 if upward else at - 1}, device_id_type=MESH,
        )

    last, first = pl.ds(ny - ROWS, ROWS), pl.ds(0, ROWS)
    halos = [
        (shift(0, "depth", me, n, vb.at[samples], vb.at[0], True), me, n, True, lambda: vb.at[0]),
        (shift(1, "depth", me, n, vb.at[1], vb.at[samples + 1], False), me, n, False, lambda: vb.at[samples + 1]),
        (shift(2, "ty", ty, n_ty, vb.at[pl.ds(1, samples), last], yup, True), ty, n_ty, True, lambda: yup),
        (shift(3, "ty", ty, n_ty, vb.at[pl.ds(1, samples), first], ydn, False), ty, n_ty, False, lambda: ydn),
        (shift(4, "tx", tx, n_tx, edge, xl, True), tx, n_tx, True, lambda: xl),
        (shift(5, "tx", tx, n_tx, edge, xr, False), tx, n_tx, False, lambda: xr),
    ]

    def send_halo(entry):
        copy, at, count, upward, place = entry
        pl.when(at < count - 1 if upward else at > 0)(copy.start)

        @pl.when(at == 0 if upward else at == count - 1)
        def _():
            place()[...] = jnp.zeros(place().shape, jnp.bfloat16)

    loads[0].wait()
    for entry in halos[:4]:
        send_halo(entry)

    group = 4
    r = lax.broadcasted_iota(jnp.int32, (nx, nx), 0)
    c = lax.broadcasted_iota(jnp.int32, (nx, nx), 1)

    def gather(step, total):
        z0 = step * group
        for k in range(group):
            hit = ((r == 0) & (c == z0 + k)) | ((r == nx - 1) & (c == samples + z0 + k))
            total = total + dot(vb[1 + z0 + k], hit.astype(jnp.float32).astype(jnp.bfloat16))
        return total

    columns = lax.fori_loop(0, samples // group, gather, jnp.zeros((ny, nx), jnp.float32))
    edge[...] = (columns[:half] + pltpu.roll(columns[half:], nx // 2, 1)).astype(jnp.bfloat16)
    for entry in halos[4:]:
        send_halo(entry)

    dy[...] = band(ny, False)

    @pl.loop(0, samples)
    def _(z):
        gy[z] = dot(dy[...], vb[1 + z])

    for copy, at, count, upward, place in halos:
        pl.when(at < count - 1 if upward else at > 0)(copy.wait_send)
        pl.when(at > 0 if upward else at < count - 1)(copy.wait_recv)

    lane = lax.broadcasted_iota(jnp.int32, (half, nx), 1)
    from_left = lax.rem(lane, nx // 2) >= samples
    held = jnp.where(from_left, xl[...].astype(jnp.float32), xr[...].astype(jnp.float32)).astype(jnp.bfloat16)
    dx = band(nx, True)
    row = lax.broadcasted_iota(jnp.int32, (ROWS, nx), 0)

    @pl.loop(0, samples)
    def _(z):
        for h in range(2):
            base = h * (nx // 2) + z
            low = ((r == base + samples) & (c == 0)).astype(jnp.float32)
            high = ((r == base) & (c == nx - 1)).astype(jnp.float32)
            rows = pl.ds(h * half, half)
            both = jnp.concatenate([vb[1 + z, rows], held], axis=1)
            weights = jnp.concatenate([dx, (high - low).astype(jnp.bfloat16)], axis=0)
            gx[z, rows] = dot(both, weights)
        above = pltpu.roll(yup[z].astype(jnp.float32), 1, 0)
        gy[z, first] = gy[z, first] - jnp.where(row == 0, above, 0.0)
        below = pltpu.roll(ydn[z].astype(jnp.float32), ROWS - 1, 0)
        gy[z, last] = gy[z, last] + jnp.where(row == ROWS - 1, below, 0.0)

    loads[1].wait()
    loads[2].wait()
    rows_each = ny // pattern.shape[1]
    slopes = [transfer[i, 0] * 0.5 for i in range(3)]
    offsets = [transfer[i, 1] * 0.5 for i in range(3)]
    slope, offset = transfer[3, 0] * LOG2E, transfer[3, 1] * LOG2E

    rank = [sum(jnp.where(order[q] == s, q, 0) for q in range(n)) for s in range(n)]
    before = [[jnp.where(rank[a] < rank[b], 1.0, 0.0) for b in range(n)] for a in range(n)]

    def part_copy(j, k, owner):
        return pltpu.make_async_remote_copy(
            src_ref=part.at[j], dst_ref=parts.at[me, k],
            send_sem=part_send.at[j], recv_sem=part_recv.at[me, k],
            device_id={"depth": owner}, device_id_type=MESH,
        )

    def fin_copy(j, k, rel):
        return pltpu.make_async_remote_copy(
            src_ref=fin.at[k], dst_ref=out.at[:, pl.ds(pl.multiple_of(j * ROWS, ROWS), ROWS)],
            send_sem=fin_send.at[k, rel - 1], recv_sem=fin_recv.at[j],
            device_id={"depth": lax.rem(me + rel, n)}, device_id_type=MESH,
        )

    def render(j):
        r0 = pl.multiple_of(j * ROWS, ROWS)
        rows = pl.ds(r0, ROWS)
        begin = start[rows]
        end = stop[rows]
        blocks = []
        for b in range(ROWS // rows_each):
            on = pattern[0, j * (ROWS // rows_each) + b, 0]
            blocks.append(jnp.where(on > 0, end[b * rows_each:(b + 1) * rows_each], 0))
        end = jnp.concatenate(blocks, axis=0)

        def layer(z, state):
            previous, v, passed, total, red, green, blue = state
            after = vb[z + 2, rows].astype(jnp.float32)
            dz = after - previous
            dyv, dxv = gy[z, rows], gx[z, rows]
            lit = jnp.abs(0.168 * dxv + 0.21 * dyv + 0.224 * dz)
            shade = 0.15 + lit * lax.rsqrt(dxv * dxv + dyv * dyv + dz * dz + 4.0)
            log = jnp.log(1.0 + jnp.exp2(v * slope + offset))
            through = jnp.exp2(log * (-scale * LOG2E))
            active = (begin <= z) & (end > z)
            now = jnp.where(active, passed * through, passed)
            weight = (passed - now) * shade
            tints = [jnp.tanh(v * slopes[i] + offsets[i]) for i in range(3)]
            return (
                v, after, now, total + weight,
                red + weight * tints[0], green + weight * tints[1], blue + weight * tints[2],
            )

        zero = jnp.zeros((ROWS, nx), jnp.float32)
        state = (
            vb[0, rows].astype(jnp.float32), vb[1, rows].astype(jnp.float32),
            jnp.ones((ROWS, nx), jnp.float32), zero, zero, zero, zero,
        )
        _, _, passed, total, red, green, blue = lax.fori_loop(0, samples, layer, state, unroll=UNROLL)
        values = (red + total, green + total, blue + total, 1.0 - passed)
        owner, k = lax.rem(j, n), j // n

        @pl.when(owner == me)
        def _():
            for i in range(4):
                parts[me, k, i] = values[i]

        @pl.when(owner != me)
        def _():
            for i in range(4):
                part[j, i] = values[i]
            part_copy(j, k, owner).start()

    def merge(j):
        owner, k = lax.rem(j, n), j // n

        @pl.when(owner == me)
        def _():
            for rel in range(1, n):
                source = lax.rem(me + rel, n)
                pltpu.make_async_remote_copy(
                    src_ref=part.at[j], dst_ref=parts.at[source, k],
                    send_sem=part_send.at[j], recv_sem=part_recv.at[source, k],
                    device_id={"depth": source}, device_id_type=MESH,
                ).wait_recv()
            hidden = [parts[s, k, 3] for s in range(n)]
            remain = 1.0 - hidden[0]
            for s in range(1, n):
                remain = remain * (1.0 - hidden[s])
            colors = [jnp.zeros_like(remain)] * 3
            for s in range(n):
                prefix = jnp.ones_like(remain)
                for a in range(n):
                    if a != s:
                        prefix = prefix * (1.0 - hidden[a] * before[a][s])
                colors = [colors[i] + prefix * parts[s, k, i] for i in range(3)]
            rows = pl.ds(pl.multiple_of(j * ROWS, ROWS), ROWS)
            for i, value in enumerate(colors + [1.0 - remain]):
                fin[k, i] = value
                out[i, rows] = value
            for rel in range(1, n):
                fin_copy(j, k, rel).start()

    @pl.loop(0, chunks + LAG)
    def _(j):
        pl.when(j < chunks)(lambda: render(j))
        pl.when(j >= LAG)(lambda: merge(j - LAG))

    @pl.loop(0, chunks)
    def _(j):
        owner, k = lax.rem(j, n), j // n

        @pl.when(owner == me)
        def _():
            for rel in range(1, n):
                fin_copy(j, k, rel).wait_send()

        @pl.when(owner != me)
        def _():
            part_copy(j, k, owner).wait_send()
            fin_copy(j, k, 1).wait_recv()


def solution(mesh):
    n, n_tx, n_ty = mesh.shape["depth"], mesh.shape["tx"], mesh.shape["ty"]

    def shards(volume, transfer, ray_start, ray_stop, pattern, depth_order):
        samples, ny, nx = volume.shape
        chunks = ny // ROWS
        owned = chunks // n
        f32, bf16 = jnp.float32, jnp.bfloat16
        any_space = pl.BlockSpec(memory_space=pl.ANY)
        smem = pl.BlockSpec(memory_space=pltpu.SMEM)
        dma = pltpu.SemaphoreType.DMA
        return pl.pallas_call(
            functools.partial(kernel, n, n_tx, n_ty, 2.0 / (samples * n)),
            out_shape=jax.ShapeDtypeStruct((4, ny, nx), f32),
            in_specs=[any_space, any_space, any_space, smem, smem, smem],
            out_specs=pl.BlockSpec(memory_space=pltpu.VMEM),
            scratch_shapes=[
                pltpu.VMEM((samples + 2, ny, nx), bf16),
                pltpu.VMEM((ny, nx), jnp.int32),
                pltpu.VMEM((ny, nx), jnp.int32),
                pltpu.VMEM((samples, ROWS, nx), bf16),
                pltpu.VMEM((samples, ROWS, nx), bf16),
                pltpu.VMEM((ny // 2, nx), bf16),
                pltpu.VMEM((ny // 2, nx), bf16),
                pltpu.VMEM((ny // 2, nx), bf16),
                pltpu.VMEM((samples, ny, nx), f32),
                pltpu.VMEM((samples, ny, nx), f32),
                pltpu.VMEM((ny, ny), bf16),
                pltpu.VMEM((chunks, 4, ROWS, nx), f32),
                pltpu.VMEM((n, owned, 4, ROWS, nx), f32),
                pltpu.VMEM((owned, 4, ROWS, nx), f32),
                dma((3,)), dma((6,)), dma((6,)),
                dma((chunks,)), dma((n, owned)), dma((owned, n - 1)), dma((chunks,)),
            ],
            compiler_params=pltpu.CompilerParams(
                collective_id=0, has_side_effects=True, vmem_limit_bytes=40 * 1024 * 1024
            ),
        )(volume, ray_start, ray_stop, pattern, transfer, depth_order)

    in_specs = (
        P("depth", "ty", "tx"),
        P(),
        P("depth", "ty", "tx"),
        P("depth", "ty", "tx"),
        P("depth", "ty", "tx"),
        P(),
    )
    return jax.shard_map(shards, mesh=mesh, in_specs=in_specs, out_specs=P(None, "ty", "tx"), check_vma=False)
```

time: 124 us -> 55.9 us (0.45); the launches traced: 122 us -> 55.7 us
  Pallas kernels: 0 us -> 49.3 us
  other arithmetic: 34.9 us -> 0 us
  waiting for transfers between devices: 21.9 us -> 0 us
  starting transfers between devices: 18.7 us -> 0 us
  local copies, waits for them, and re-layouts: 22.5 us -> 6.35 us
  blocking collectives: 15.9 us -> 0 us
  loops' own time: 7.94 us -> 0 us
    pallas_call x0 -> x1, Pallas kernels: none -> 49.3 us  [shards(): pl.pallas_call(functools.partial(kernel, n, n_tx, n_ty, 2.0 / (samples *...]
    all_gather x1 -> x0, blocking collectives: 15.9 us -> none  [shards(): return lax.all_gather(picture, 'depth', axis=1, tiled=True)]
    ppermute x6 -> x0, starting transfers between devices: 14.9 us -> none  [the longest x3 10.8 us: with_halo(): before = lax.ppermute(last, axis, up)]
    all_to_all x1 -> x0, waiting for transfers between devices: 13.7 us -> none  [shards(): lax.all_to_all(stacked, 'depth', split_axis=2, concat_axis=0, tiled=True)]
    mul x5 -> x0, other arithmetic: 13.5 us -> none  [the longest x1 13.5 us: local_partial(): weights = prior * opacity * shading]
    slice x5 -> x0, local copies, waits for them, and re-layouts: 10.1 us -> none  [the longest x1 4.97 us: with_halo(): last = lax.slice_in_dim(array, length - width, length, axis=dim)]
    ppermute x6 -> x0, waiting for transfers between devices: 8.15 us -> none  [the longest x3 5.69 us: with_halo(): after = lax.ppermute(initial, axis, down)]
    another operation x1 -> x0, loops' own time: 7.94 us -> none  [composite(): colors, remain = lax.fori_loop(0, count, step, start_pair)]
  transfers between devices with their start and end apart: 7 -> 0, of which waited for: 5 -> 0; matrix products, arithmetic and copies ran while one was open for 4% -> 0% of each run, Pallas kernels for 0% -> 0%
where the time goes in v1:
time: 55.9 us; the launch traced here: 55.7 us
  Pallas kernels  49.3 us (88%)
  local copies, waits for them, and re-layouts  6.35 us (11%)
    pallas_call x1, Pallas kernels, shards(): pl.pallas_call(functools.partial(kernel, n, n_tx, n_ty, 2.0 / (samples *...  49.3 us
    unnamed x11, local copies, waits for them, and re-layouts  6.35 us

profile of v1, /device:TPU:0, one launch (start us, length us, event | category | flops | bytes accessed | tf_op | source)
XLA Modules:
  0.0 55.7 jit_solution(16120136970219426762)
XLA Ops:
  0.0 0.8 %copy.8.transfer = f32[4,2]{1,0:T(4,128)S(1)} copy(f32[4,2]{0,1:T(2,128)} %param.7) | data formatting | bytes 64 | tf_op args[1]
  0.8 0.7 %copy.7.pattern = s32[1,32,1]{2,1,0:T(8,128)S(1)} copy(s32[1,32,1]{1,2,0:T(1,128)} %param.10) | data formatting | bytes 256 | tf_op args[4]
  1.5 0.0 copy-start
  1.5 1.6 %copy-done = bf16[32,256,128]{2,1,0:T(8,128)(2,1)S(1)} copy-done((bf16[32,256,128]{2,1,0:T(8,128)(2,1)S(1)}, bf16[32,256,128]{2,1,0:T(8,128)(2,1)}, u32[]{:S(2)}) %copy-start) | copy-done | bytes 2097176
  3.1 0.0 copy-start.1
  3.1 0.9 %copy-done.1 = s32[1,256,128]{2,1,0:T(8,128)S(1)} copy-done((s32[1,256,128]{2,1,0:T(8,128)S(1)}, s32[1,256,128]{2,1,0:T(8,128)}, u32[]{:S(2)}) %copy-start.1) | copy-done | bytes 131096
  4.0 0.0 copy-start.2
  4.0 0.9 %copy-done.2 = s32[1,256,128]{2,1,0:T(8,128)S(1)} copy-done((s32[1,256,128]{2,1,0:T(8,128)S(1)}, s32[1,256,128]{2,1,0:T(8,128)}, u32[]{:S(2)}) %copy-start.2) | copy-done | bytes 131096
  4.9 0.0 copy-start.3
  4.9 0.7 %copy-done.3 = s32[4]{0:T(128)S(1)} copy-done((s32[4]{0:T(128)S(1)}, s32[4]{0:T(128)}, u32[]{:S(2)}) %copy-start.3) | copy-done | bytes 40
  5.6 49.3 %shard_map.64 = f32[4,256,128]{2,1,0:T(8,128)S(1)} custom-call(bf16[32,256,128]{2,1,0:T(8,128)(2,1)S(1)} %copy-done, s32[1,256,128]{2,1,0:T(8,128)S(1)} %copy-done.1, s32[1,256,128]{2,1,0:T(8,128)S(1)} %copy-done.2, s32[1,32,1]{2,1,0:T(8,128)S(1)} %copy.7.pattern, f32[4,2]{1,0:T(4,128)S(1)} %copy.8.transfer, s32[4]{0:T(128)S(1)} %copy-done.3), custom_call_target="tpu_custom_call" | custom-call | tf_op jit(solution)/shard_map/pallas_call | solution.py:275
  54.9 0.8 %copy.10 = f32[4,256,128]{2,1,0:T(8,128)} copy(f32[4,256,128]{2,1,0:T(8,128)S(1)} %shard_map.64) | data formatting | bytes 1048576
Async XLA Ops:
  1.5 1.6 %copy-start = (bf16[32,256,128]{2,1,0:T(8,128)(2,1)S(1)}, bf16[32,256,128]{2,1,0:T(8,128)(2,1)}, u32[]{:S(2)}) copy-start(bf16[32,256,128]{2,1,0:T(8,128)(2,1)} %vol.1) | copy-start | bytes 6291460
  3.1 0.9 %copy-start.1 = (s32[1,256,128]{2,1,0:T(8,128)S(1)}, s32[1,256,128]{2,1,0:T(8,128)}, u32[]{:S(2)}) copy-start(s32[1,256,128]{2,1,0:T(8,128)} %start_hbm.1) | copy-start | bytes 393220
  4.0 0.9 %copy-start.2 = (s32[1,256,128]{2,1,0:T(8,128)S(1)}, s32[1,256,128]{2,1,0:T(8,128)}, u32[]{:S(2)}) copy-start(s32[1,256,128]{2,1,0:T(8,128)} %stop_hbm.1) | copy-start | bytes 393220
  4.9 0.7 %copy-start.3 = (s32[4]{0:T(128)S(1)}, s32[4]{0:T(128)}, u32[]{:S(2)}) copy-start(s32[4]{0:T(128)} %order.1) | copy-start | bytes 52

commit v2 on v1

--- a/solution.py
+++ b/solution.py
@@ -13,13 +13,19 @@
 LAG = 5
 UNROLL = 8
 LOG2E = math.log2(math.e)
-
-
-def band(length, across):
-    r = lax.broadcasted_iota(jnp.int32, (length, length), 0)
-    c = lax.broadcasted_iota(jnp.int32, (length, length), 1)
-    up, down = (r == c + 1, r + 1 == c) if across else (c == r + 1, c + 1 == r)
-    return (up.astype(jnp.float32) - down.astype(jnp.float32)).astype(jnp.bfloat16)
+OCTAVES = 22
+CODES = 65535.0 / OCTAVES
+
+
+def encode(x):
+    place = jnp.log(jnp.clip(x, 1e-30, 1.0)) * (CODES * LOG2E) + 65535.5
+    return (jnp.maximum(place, 0.0).astype(jnp.int32) - 32768).astype(jnp.int16)
+
+
+def decode(code):
+    wide = code.astype(jnp.int32)
+    value = jnp.exp2((wide.astype(jnp.float32) - 32767.0) * (1.0 / CODES))
+    return jnp.where(wide == -32768, 0.0, value)
 
 
 def dot(a, b):
@@ -29,7 +35,7 @@
 def kernel(
     n, n_tx, n_ty, scale,
     vol, start_hbm, stop_hbm, pattern, transfer, order, out,
-    vb, start, stop, yup, ydn, edge, xl, xr, gx, gy, dy, part, parts, fin,
+    vb, start, stop, yup, ydn, edge, xl, xr, vf, held, part, parts, fin,
     load_sem, halo_send, halo_recv, part_send, part_recv, fin_send, fin_recv,
 ):
     samples, ny, nx = vol.shape
@@ -98,7 +104,8 @@
     def gather(step, total):
         z0 = step * group
         for k in range(group):
-            hit = ((r == 0) & (c == z0 + k)) | ((r == nx - 1) & (c == samples + z0 + k))
+            lane = 2 * (z0 + k)
+            hit = ((r == nx - 1) & (c == lane)) | ((r == 0) & (c == lax.rem(lane + nx - 1, nx)))
             total = total + dot(vb[1 + z0 + k], hit.astype(jnp.float32).astype(jnp.bfloat16))
         return total
 
@@ -107,43 +114,32 @@
     for entry in halos[4:]:
         send_halo(entry)
 
-    dy[...] = band(ny, False)
+    body = pl.ds(8, ny)
 
     @pl.loop(0, samples)
     def _(z):
-        gy[z] = dot(dy[...], vb[1 + z])
+        vf[1 + z, body] = vb[1 + z].astype(jnp.float32)
 
     for copy, at, count, upward, place in halos:
         pl.when(at < count - 1 if upward else at > 0)(copy.wait_send)
         pl.when(at > 0 if upward else at < count - 1)(copy.wait_recv)
 
     lane = lax.broadcasted_iota(jnp.int32, (half, nx), 1)
-    from_left = lax.rem(lane, nx // 2) >= samples
-    held = jnp.where(from_left, xl[...].astype(jnp.float32), xr[...].astype(jnp.float32)).astype(jnp.bfloat16)
-    dx = band(nx, True)
-    row = lax.broadcasted_iota(jnp.int32, (ROWS, nx), 0)
+    held[...] = jnp.where(lax.rem(lane, 2) == 0, xl[...].astype(jnp.float32), xr[...].astype(jnp.float32))
+    for z in (0, samples + 1):
+        vf[z, body] = vb[z].astype(jnp.float32)
 
     @pl.loop(0, samples)
     def _(z):
-        for h in range(2):
-            base = h * (nx // 2) + z
-            low = ((r == base + samples) & (c == 0)).astype(jnp.float32)
-            high = ((r == base) & (c == nx - 1)).astype(jnp.float32)
-            rows = pl.ds(h * half, half)
-            both = jnp.concatenate([vb[1 + z, rows], held], axis=1)
-            weights = jnp.concatenate([dx, (high - low).astype(jnp.bfloat16)], axis=0)
-            gx[z, rows] = dot(both, weights)
-        above = pltpu.roll(yup[z].astype(jnp.float32), 1, 0)
-        gy[z, first] = gy[z, first] - jnp.where(row == 0, above, 0.0)
-        below = pltpu.roll(ydn[z].astype(jnp.float32), ROWS - 1, 0)
-        gy[z, last] = gy[z, last] + jnp.where(row == ROWS - 1, below, 0.0)
+        vf[1 + z, pl.ds(0, 8)] = yup[z].astype(jnp.float32)[ROWS - 8:]
+        vf[1 + z, pl.ds(8 + ny, 8)] = ydn[z].astype(jnp.float32)[:8]
 
     loads[1].wait()
     loads[2].wait()
     rows_each = ny // pattern.shape[1]
-    slopes = [transfer[i, 0] * 0.5 for i in range(3)]
-    offsets = [transfer[i, 1] * 0.5 for i in range(3)]
-    slope, offset = transfer[3, 0] * LOG2E, transfer[3, 1] * LOG2E
+    slopes = [transfer[0, i] * 0.5 for i in range(3)]
+    offsets = [transfer[1, i] * 0.5 for i in range(3)]
+    slope, offset = transfer[0, 3] * LOG2E, transfer[1, 3] * LOG2E
 
     rank = [sum(jnp.where(order[q] == s, q, 0) for q in range(n)) for s in range(n)]
     before = [[jnp.where(rank[a] < rank[b], 1.0, 0.0) for b in range(n)] for a in range(n)]
@@ -169,15 +165,19 @@
         end = stop[rows]
         blocks = []
         for b in range(ROWS // rows_each):
-            on = pattern[0, j * (ROWS // rows_each) + b, 0]
+            on = pattern[0, j * (ROWS // rows_each) + b]
             blocks.append(jnp.where(on > 0, end[b * rows_each:(b + 1) * rows_each], 0))
         end = jnp.concatenate(blocks, axis=0)
 
         def layer(z, state):
             previous, v, passed, total, red, green, blue = state
-            after = vb[z + 2, rows].astype(jnp.float32)
+            after = vf[z + 2, pl.ds(pl.multiple_of(r0 + 8, 8), ROWS)]
+            near = vf.at[z + 1, pl.ds(r0, ROWS + 16)]
             dz = after - previous
-            dyv, dxv = gy[z, rows], gx[z, rows]
+            dyv = near[pl.ds(9, ROWS)] - near[pl.ds(7, ROWS)]
+            beside = pltpu.roll(sides_of, lax.rem(nx - 2 * z, nx), 1)
+            right = jnp.where(lane == nx - 1, beside, pltpu.roll(v, nx - 1, 1))
+            dxv = right - jnp.where(lane == 0, beside, pltpu.roll(v, 1, 1))
             lit = jnp.abs(0.168 * dxv + 0.21 * dyv + 0.224 * dz)
             shade = 0.15 + lit * lax.rsqrt(dxv * dxv + dyv * dyv + dz * dz + 4.0)
             log = jnp.log(1.0 + jnp.exp2(v * slope + offset))
@@ -191,13 +191,18 @@
                 red + weight * tints[0], green + weight * tints[1], blue + weight * tints[2],
             )
 
+        upper = j * ROWS // half
+        sides_of = held[pl.ds(pl.multiple_of(r0 - upper * half, ROWS), ROWS)]
+        sides_of = pltpu.roll(sides_of, upper * (nx // 2), 1)
+        lane = lax.broadcasted_iota(jnp.int32, (ROWS, nx), 1)
         zero = jnp.zeros((ROWS, nx), jnp.float32)
+        inner = pl.ds(pl.multiple_of(r0 + 8, 8), ROWS)
         state = (
-            vb[0, rows].astype(jnp.float32), vb[1, rows].astype(jnp.float32),
+            vf[0, inner], vf[1, inner],
             jnp.ones((ROWS, nx), jnp.float32), zero, zero, zero, zero,
         )
         _, _, passed, total, red, green, blue = lax.fori_loop(0, samples, layer, state, unroll=UNROLL)
-        values = (red + total, green + total, blue + total, 1.0 - passed)
+        values = [encode(x) for x in (red + total, green + total, blue + total, 1.0 - passed)]
         owner, k = lax.rem(j, n), j // n
 
         @pl.when(owner == me)
@@ -223,7 +228,7 @@
                     send_sem=part_send.at[j], recv_sem=part_recv.at[source, k],
                     device_id={"depth": source}, device_id_type=MESH,
                 ).wait_recv()
-            hidden = [parts[s, k, 3] for s in range(n)]
+            hidden = [decode(parts[s, k, 3]) for s in range(n)]
             remain = 1.0 - hidden[0]
             for s in range(1, n):
                 remain = remain * (1.0 - hidden[s])
@@ -233,11 +238,11 @@
                 for a in range(n):
                     if a != s:
                         prefix = prefix * (1.0 - hidden[a] * before[a][s])
-                colors = [colors[i] + prefix * parts[s, k, i] for i in range(3)]
+                colors = [colors[i] + prefix * decode(parts[s, k, i]) for i in range(3)]
             rows = pl.ds(pl.multiple_of(j * ROWS, ROWS), ROWS)
             for i, value in enumerate(colors + [1.0 - remain]):
-                fin[k, i] = value
-                out[i, rows] = value
+                fin[k, i] = encode(value)
+                out[i, rows] = encode(value)
             for rel in range(1, n):
                 fin_copy(j, k, rel).start()
 
@@ -268,13 +273,13 @@
         samples, ny, nx = volume.shape
         chunks = ny // ROWS
         owned = chunks // n
-        f32, bf16 = jnp.float32, jnp.bfloat16
+        f32, bf16, i16 = jnp.float32, jnp.bfloat16, jnp.int16
         any_space = pl.BlockSpec(memory_space=pl.ANY)
         smem = pl.BlockSpec(memory_space=pltpu.SMEM)
         dma = pltpu.SemaphoreType.DMA
-        return pl.pallas_call(
+        codes = pl.pallas_call(
             functools.partial(kernel, n, n_tx, n_ty, 2.0 / (samples * n)),
-            out_shape=jax.ShapeDtypeStruct((4, ny, nx), f32),
+            out_shape=jax.ShapeDtypeStruct((4, ny, nx), i16),
             in_specs=[any_space, any_space, any_space, smem, smem, smem],
             out_specs=pl.BlockSpec(memory_space=pltpu.VMEM),
             scratch_shapes=[
@@ -286,19 +291,19 @@
                 pltpu.VMEM((ny // 2, nx), bf16),
                 pltpu.VMEM((ny // 2, nx), bf16),
                 pltpu.VMEM((ny // 2, nx), bf16),
-                pltpu.VMEM((samples, ny, nx), f32),
-                pltpu.VMEM((samples, ny, nx), f32),
-                pltpu.VMEM((ny, ny), bf16),
-                pltpu.VMEM((chunks, 4, ROWS, nx), f32),
-                pltpu.VMEM((n, owned, 4, ROWS, nx), f32),
-                pltpu.VMEM((owned, 4, ROWS, nx), f32),
+                pltpu.VMEM((samples + 2, ny + 16, nx), f32),
+                pltpu.VMEM((ny // 2, nx), f32),
+                pltpu.VMEM((chunks, 4, ROWS, nx), i16),
+                pltpu.VMEM((n, owned, 4, ROWS, nx), i16),
+                pltpu.VMEM((owned, 4, ROWS, nx), i16),
                 dma((3,)), dma((6,)), dma((6,)),
                 dma((chunks,)), dma((n, owned)), dma((owned, n - 1)), dma((chunks,)),
             ],
             compiler_params=pltpu.CompilerParams(
-                collective_id=0, has_side_effects=True, vmem_limit_bytes=40 * 1024 * 1024
+                collective_id=0, has_side_effects=True, vmem_limit_bytes=62 * 1024 * 1024
             ),
-        )(volume, ray_start, ray_stop, pattern, transfer, depth_order)
+        )(volume, ray_start, ray_stop, pattern[:, :, 0], transfer.T, depth_order)
+        return decode(codes)
 
     in_specs = (
         P("depth", "ty", "tx"),

time: 55.9 us -> 34.4 us (0.62)
  Pallas kernels: 49.3 us -> 32.3 us
  local copies, waits for them, and re-layouts: 6.35 us -> 0 us
  other arithmetic: 0 us -> 1.92 us
    pallas_call x1, Pallas kernels: 49.3 us -> 32.3 us  [shards(): pl.pallas_call(functools.partial(kernel, n, n_tx, n_ty, 2.0 / (samples *...]
    unnamed x11 -> x0, local copies, waits for them, and re-layouts: 6.35 us -> none
    select_n x0 -> x1, other arithmetic: none -> 1.92 us  [decode(): return jnp.where(wide == -32768, 0.0, value)]
where the time goes in v2:
time: 34.4 us; the launch traced here: 34.2 us
  Pallas kernels  32.3 us (94%)
  other arithmetic  1.92 us (6%)
    pallas_call x1, Pallas kernels, shards(): pl.pallas_call(functools.partial(kernel, n, n_tx, n_ty, 2.0 / (samples *...  32.3 us
    select_n x1, other arithmetic, decode(): return jnp.where(wide == -32768, 0.0, value)  1.92 us

profile of v2, /device:TPU:0, one launch (start us, length us, event | category | flops | bytes accessed | tf_op | source)
XLA Modules:
  0.0 34.2 jit_solution(10937760531080324594)
XLA Ops:
  0.0 32.3 %shard_map.64 = s16[4,256,128]{2,1,0:T(8,128)(2,1)} custom-call(bf16[32,256,128]{2,1,0:T(8,128)(2,1)} %vol.1, s32[1,256,128]{2,1,0:T(8,128)} %start_hbm.1, s32[1,256,128]{2,1,0:T(8,128)} %stop_hbm.1, s32[1,32]{1,0:T(1,128)} %bitcast.3, f32[2,4]{1,0:T(2,128)} %bitcast.2, s32[4]{0:T(128)} %order.1), custom_call_target="tpu_custom_call" | custom-call | tf_op jit(solution)/shard_map/pallas_call | solution.py:280
  32.3 1.9 %fusion.3 = f32[4,256,128]{2,1,0:T(8,128)} fusion(s16[4,256,128]{2,1,0:T(8,128)(2,1)} %shard_map.64), kind=kLoop, calls=%fused_computation.5 | loop fusion | flops 786432 | bytes 786432 | tf_op jit(solution)/shard_map/jit(_where)/select_n | solution.py:28

commit v3 on v2

--- a/solution.py
+++ b/solution.py
@@ -9,9 +9,9 @@
 from jax.sharding import PartitionSpec as P
 
 MESH = pl.DeviceIdType.MESH
-ROWS = 16
-LAG = 5
-UNROLL = 8
+STRIP = 16
+LAG_ROWS = 224
+UNROLL = 16
 LOG2E = math.log2(math.e)
 OCTAVES = 22
 CODES = 65535.0 / OCTAVES
@@ -33,15 +33,15 @@
 
 
 def kernel(
-    n, n_tx, n_ty, scale,
+    n, n_tx, n_ty, scale, each,
     vol, start_hbm, stop_hbm, pattern, transfer, order, out,
-    vb, start, stop, yup, ydn, edge, xl, xr, vf, held, part, parts, fin,
+    vb, start, stop, yup, ydn, edge, xl, xr, vf, share, held, part, parts, fin,
     load_sem, halo_send, halo_recv, part_send, part_recv, fin_send, fin_recv,
 ):
     samples, ny, nx = vol.shape
     half = ny // 2
-    chunks = ny // ROWS
-    owned = chunks // n
+    chunks = ny // each
+    lag = LAG_ROWS // each
     tx, ty, me = lax.axis_index("tx"), lax.axis_index("ty"), lax.axis_index("depth")
 
     loads = [
@@ -75,7 +75,7 @@
             device_id={axis: at + 1 if upward else at - 1}, device_id_type=MESH,
         )
 
-    last, first = pl.ds(ny - ROWS, ROWS), pl.ds(0, ROWS)
+    last, first = pl.ds(ny - STRIP, STRIP), pl.ds(0, STRIP)
     halos = [
         (shift(0, "depth", me, n, vb.at[samples], vb.at[0], True), me, n, True, lambda: vb.at[0]),
         (shift(1, "depth", me, n, vb.at[1], vb.at[samples + 1], False), me, n, False, lambda: vb.at[samples + 1]),
@@ -103,11 +103,13 @@
 
     def gather(step, total):
         z0 = step * group
+        hits = []
         for k in range(group):
             lane = 2 * (z0 + k)
             hit = ((r == nx - 1) & (c == lane)) | ((r == 0) & (c == lax.rem(lane + nx - 1, nx)))
-            total = total + dot(vb[1 + z0 + k], hit.astype(jnp.float32).astype(jnp.bfloat16))
-        return total
+            hits.append(hit.astype(jnp.float32).astype(jnp.bfloat16))
+        layers = jnp.concatenate([vb[1 + z0 + k] for k in range(group)], axis=1)
+        return total + dot(layers, jnp.concatenate(hits, axis=0))
 
     columns = lax.fori_loop(0, samples // group, gather, jnp.zeros((ny, nx), jnp.float32))
     edge[...] = (columns[:half] + pltpu.roll(columns[half:], nx // 2, 1)).astype(jnp.bfloat16)
@@ -115,24 +117,6 @@
         send_halo(entry)
 
     body = pl.ds(8, ny)
-
-    @pl.loop(0, samples)
-    def _(z):
-        vf[1 + z, body] = vb[1 + z].astype(jnp.float32)
-
-    for copy, at, count, upward, place in halos:
-        pl.when(at < count - 1 if upward else at > 0)(copy.wait_send)
-        pl.when(at > 0 if upward else at < count - 1)(copy.wait_recv)
-
-    lane = lax.broadcasted_iota(jnp.int32, (half, nx), 1)
-    held[...] = jnp.where(lax.rem(lane, 2) == 0, xl[...].astype(jnp.float32), xr[...].astype(jnp.float32))
-    for z in (0, samples + 1):
-        vf[z, body] = vb[z].astype(jnp.float32)
-
-    @pl.loop(0, samples)
-    def _(z):
-        vf[1 + z, pl.ds(0, 8)] = yup[z].astype(jnp.float32)[ROWS - 8:]
-        vf[1 + z, pl.ds(8 + ny, 8)] = ydn[z].astype(jnp.float32)[:8]
 
     loads[1].wait()
     loads[2].wait()
@@ -144,6 +128,58 @@
     rank = [sum(jnp.where(order[q] == s, q, 0) for q in range(n)) for s in range(n)]
     before = [[jnp.where(rank[a] < rank[b], 1.0, 0.0) for b in range(n)] for a in range(n)]
 
+    def owner_of(j):
+        turn = lax.rem(j, n)
+        return jnp.where(lax.rem(turn, 2) == 0, turn // 2, n - 1 - turn // 2)
+
+    @pl.loop(0, chunks)
+    def _(j):
+        r0 = pl.multiple_of(j * each, each)
+        rows, inner = pl.ds(r0, each), pl.ds(pl.multiple_of(r0 + 8, 8), each)
+        begin = start[rows]
+        end = stop[rows]
+        blocks = []
+        for b in range(each // rows_each):
+            on = pattern[0, j * (each // rows_each) + b]
+            blocks.append(jnp.where(on > 0, end[b * rows_each:(b + 1) * rows_each], 0))
+        end = jnp.concatenate(blocks, axis=0)
+
+        def layer(z, passed):
+            v = vb[z + 1, rows].astype(jnp.float32)
+            vf[z + 1, inner] = v
+            log = jnp.log(1.0 + jnp.exp2(v * slope + offset))
+            through = jnp.exp2(log * (-scale * LOG2E))
+            active = (begin <= z) & (end > z)
+            now = jnp.where(active, passed * through, passed)
+            share[z, rows] = passed - now
+            return now
+
+        passed = lax.fori_loop(0, samples, layer, jnp.ones((each, nx), jnp.float32), unroll=UNROLL)
+        hidden = encode(1.0 - passed)
+        owner, k = owner_of(j), j // n
+
+        @pl.when(owner == me)
+        def _():
+            parts[me, k, 3] = hidden
+
+        @pl.when(owner != me)
+        def _():
+            part[j, 3] = hidden
+
+    for copy, at, count, upward, place in halos:
+        pl.when(at < count - 1 if upward else at > 0)(copy.wait_send)
+        pl.when(at > 0 if upward else at < count - 1)(copy.wait_recv)
+
+    lane = lax.broadcasted_iota(jnp.int32, (half, nx), 1)
+    held[...] = jnp.where(lax.rem(lane, 2) == 0, xl[...].astype(jnp.float32), xr[...].astype(jnp.float32))
+    for z in (0, samples + 1):
+        vf[z, body] = vb[z].astype(jnp.float32)
+
+    @pl.loop(0, samples)
+    def _(z):
+        vf[1 + z, pl.ds(0, 8)] = yup[z].astype(jnp.float32)[STRIP - 8:]
+        vf[1 + z, pl.ds(8 + ny, 8)] = ydn[z].astype(jnp.float32)[:8]
+
     def part_copy(j, k, owner):
         return pltpu.make_async_remote_copy(
             src_ref=part.at[j], dst_ref=parts.at[me, k],
@@ -153,71 +189,59 @@
 
     def fin_copy(j, k, rel):
         return pltpu.make_async_remote_copy(
-            src_ref=fin.at[k], dst_ref=out.at[:, pl.ds(pl.multiple_of(j * ROWS, ROWS), ROWS)],
+            src_ref=fin.at[k], dst_ref=out.at[:, pl.ds(pl.multiple_of(j * each, each), each)],
             send_sem=fin_send.at[k, rel - 1], recv_sem=fin_recv.at[j],
             device_id={"depth": lax.rem(me + rel, n)}, device_id_type=MESH,
         )
 
     def render(j):
-        r0 = pl.multiple_of(j * ROWS, ROWS)
-        rows = pl.ds(r0, ROWS)
-        begin = start[rows]
-        end = stop[rows]
-        blocks = []
-        for b in range(ROWS // rows_each):
-            on = pattern[0, j * (ROWS // rows_each) + b]
-            blocks.append(jnp.where(on > 0, end[b * rows_each:(b + 1) * rows_each], 0))
-        end = jnp.concatenate(blocks, axis=0)
-
+        r0 = pl.multiple_of(j * each, each)
+        rows = pl.ds(r0, each)
         def layer(z, state):
-            previous, v, passed, total, red, green, blue = state
-            after = vf[z + 2, pl.ds(pl.multiple_of(r0 + 8, 8), ROWS)]
-            near = vf.at[z + 1, pl.ds(r0, ROWS + 16)]
+            previous, v, total, red, green, blue = state
+            after = vf[z + 2, pl.ds(pl.multiple_of(r0 + 8, 8), each)]
+            near = vf.at[z + 1, pl.ds(r0, each + 16)]
             dz = after - previous
-            dyv = near[pl.ds(9, ROWS)] - near[pl.ds(7, ROWS)]
+            dyv = near[pl.ds(9, each)] - near[pl.ds(7, each)]
             beside = pltpu.roll(sides_of, lax.rem(nx - 2 * z, nx), 1)
             right = jnp.where(lane == nx - 1, beside, pltpu.roll(v, nx - 1, 1))
             dxv = right - jnp.where(lane == 0, beside, pltpu.roll(v, 1, 1))
             lit = jnp.abs(0.168 * dxv + 0.21 * dyv + 0.224 * dz)
             shade = 0.15 + lit * lax.rsqrt(dxv * dxv + dyv * dyv + dz * dz + 4.0)
-            log = jnp.log(1.0 + jnp.exp2(v * slope + offset))
-            through = jnp.exp2(log * (-scale * LOG2E))
-            active = (begin <= z) & (end > z)
-            now = jnp.where(active, passed * through, passed)
-            weight = (passed - now) * shade
+            weight = share[z, rows] * shade
             tints = [jnp.tanh(v * slopes[i] + offsets[i]) for i in range(3)]
             return (
-                v, after, now, total + weight,
+                v, after, total + weight,
                 red + weight * tints[0], green + weight * tints[1], blue + weight * tints[2],
             )
 
-        upper = j * ROWS // half
-        sides_of = held[pl.ds(pl.multiple_of(r0 - upper * half, ROWS), ROWS)]
+        upper = j * each // half
+        sides_of = held[pl.ds(pl.multiple_of(r0 - upper * half, each), each)]
         sides_of = pltpu.roll(sides_of, upper * (nx // 2), 1)
-        lane = lax.broadcasted_iota(jnp.int32, (ROWS, nx), 1)
-        zero = jnp.zeros((ROWS, nx), jnp.float32)
-        inner = pl.ds(pl.multiple_of(r0 + 8, 8), ROWS)
+        lane = lax.broadcasted_iota(jnp.int32, (each, nx), 1)
+        zero = jnp.zeros((each, nx), jnp.float32)
+        inner = pl.ds(pl.multiple_of(r0 + 8, 8), each)
         state = (
             vf[0, inner], vf[1, inner],
-            jnp.ones((ROWS, nx), jnp.float32), zero, zero, zero, zero,
+            zero, zero, zero, zero,
         )
-        _, _, passed, total, red, green, blue = lax.fori_loop(0, samples, layer, state, unroll=UNROLL)
-        values = [encode(x) for x in (red + total, green + total, blue + total, 1.0 - passed)]
-        owner, k = lax.rem(j, n), j // n
+        _, _, total, red, green, blue = lax.fori_loop(0, samples, layer, state, unroll=UNROLL)
+        values = [encode(x) for x in (red + total, green + total, blue + total)]
+        owner, k = owner_of(j), j // n
 
         @pl.when(owner == me)
         def _():
-            for i in range(4):
+            for i in range(3):
                 parts[me, k, i] = values[i]
 
         @pl.when(owner != me)
         def _():
-            for i in range(4):
+            for i in range(3):
                 part[j, i] = values[i]
             part_copy(j, k, owner).start()
 
     def merge(j):
-        owner, k = lax.rem(j, n), j // n
+        owner, k = owner_of(j), j // n
 
         @pl.when(owner == me)
         def _():
@@ -239,21 +263,21 @@
                     if a != s:
                         prefix = prefix * (1.0 - hidden[a] * before[a][s])
                 colors = [colors[i] + prefix * decode(parts[s, k, i]) for i in range(3)]
-            rows = pl.ds(pl.multiple_of(j * ROWS, ROWS), ROWS)
+            rows = pl.ds(pl.multiple_of(j * each, each), each)
             for i, value in enumerate(colors + [1.0 - remain]):
                 fin[k, i] = encode(value)
                 out[i, rows] = encode(value)
             for rel in range(1, n):
                 fin_copy(j, k, rel).start()
 
-    @pl.loop(0, chunks + LAG)
+    @pl.loop(0, chunks + lag)
     def _(j):
         pl.when(j < chunks)(lambda: render(j))
-        pl.when(j >= LAG)(lambda: merge(j - LAG))
+        pl.when(j >= lag)(lambda: merge(j - lag))
 
     @pl.loop(0, chunks)
     def _(j):
-        owner, k = lax.rem(j, n), j // n
+        owner, k = owner_of(j), j // n
 
         @pl.when(owner == me)
         def _():
@@ -271,14 +295,15 @@
 
     def shards(volume, transfer, ray_start, ray_stop, pattern, depth_order):
         samples, ny, nx = volume.shape
-        chunks = ny // ROWS
+        rows = min(32, ny // n)
+        chunks = ny // rows
         owned = chunks // n
         f32, bf16, i16 = jnp.float32, jnp.bfloat16, jnp.int16
         any_space = pl.BlockSpec(memory_space=pl.ANY)
         smem = pl.BlockSpec(memory_space=pltpu.SMEM)
         dma = pltpu.SemaphoreType.DMA
         codes = pl.pallas_call(
-            functools.partial(kernel, n, n_tx, n_ty, 2.0 / (samples * n)),
+            functools.partial(kernel, n, n_tx, n_ty, 2.0 / (samples * n), rows),
             out_shape=jax.ShapeDtypeStruct((4, ny, nx), i16),
             in_specs=[any_space, any_space, any_space, smem, smem, smem],
             out_specs=pl.BlockSpec(memory_space=pltpu.VMEM),
@@ -286,16 +311,17 @@
                 pltpu.VMEM((samples + 2, ny, nx), bf16),
                 pltpu.VMEM((ny, nx), jnp.int32),
                 pltpu.VMEM((ny, nx), jnp.int32),
-                pltpu.VMEM((samples, ROWS, nx), bf16),
-                pltpu.VMEM((samples, ROWS, nx), bf16),
+                pltpu.VMEM((samples, STRIP, nx), bf16),
+                pltpu.VMEM((samples, STRIP, nx), bf16),
                 pltpu.VMEM((ny // 2, nx), bf16),
                 pltpu.VMEM((ny // 2, nx), bf16),
                 pltpu.VMEM((ny // 2, nx), bf16),
                 pltpu.VMEM((samples + 2, ny + 16, nx), f32),
+                pltpu.VMEM((samples, ny, nx), f32),
                 pltpu.VMEM((ny // 2, nx), f32),
-                pltpu.VMEM((chunks, 4, ROWS, nx), i16),
-                pltpu.VMEM((n, owned, 4, ROWS, nx), i16),
-                pltpu.VMEM((owned, 4, ROWS, nx), i16),
+                pltpu.VMEM((chunks, 4, rows, nx), i16),
+                pltpu.VMEM((n, owned, 4, rows, nx), i16),
+                pltpu.VMEM((owned, 4, rows, nx), i16),
                 dma((3,)), dma((6,)), dma((6,)),
                 dma((chunks,)), dma((n, owned)), dma((owned, n - 1)), dma((chunks,)),
             ],

time: 34.4 us -> 28.6 us (0.83)
  Pallas kernels: 32.3 us -> 26.5 us
    pallas_call x1, Pallas kernels: 32.3 us -> 26.5 us  [shards(): pl.pallas_call(functools.partial(kernel, n, n_tx, n_ty, 2.0 / (samples *...]
where the time goes in v3:
time: 28.6 us; the launch traced here: 28.5 us
  Pallas kernels  26.5 us (93%)
  other arithmetic  1.92 us (7%)
    pallas_call x1, Pallas kernels, shards(): pl.pallas_call(functools.partial(kernel, n, n_tx, n_ty, 2.0 / (samples *...  26.5 us
    select_n x1, other arithmetic, decode(): return jnp.where(wide == -32768, 0.0, value)  1.92 us

profile of v3, /device:TPU:0, one launch (start us, length us, event | category | flops | bytes accessed | tf_op | source)
XLA Modules:
  0.0 28.5 jit_solution(14901500601235026630)
XLA Ops:
  0.0 26.5 %shard_map.64 = s16[4,256,128]{2,1,0:T(8,128)(2,1)} custom-call(bf16[32,256,128]{2,1,0:T(8,128)(2,1)} %vol.1, s32[1,256,128]{2,1,0:T(8,128)} %start_hbm.1, s32[1,256,128]{2,1,0:T(8,128)} %stop_hbm.1, s32[1,32]{1,0:T(1,128)} %bitcast.3, f32[2,4]{1,0:T(2,128)} %bitcast.2, s32[4]{0:T(128)} %order.1), custom_call_target="tpu_custom_call" | custom-call | tf_op jit(solution)/shard_map/pallas_call | solution.py:305
  26.5 1.9 %fusion.3 = f32[4,256,128]{2,1,0:T(8,128)} fusion(s16[4,256,128]{2,1,0:T(8,128)(2,1)} %shard_map.64), kind=kLoop, calls=%fused_computation.5 | loop fusion | flops 786432 | bytes 786432 | tf_op jit(solution)/shard_map/jit(_where)/select_n | solution.py:28

commit v4 on v3

--- a/solution.py
+++ b/solution.py
@@ -11,7 +11,7 @@
 MESH = pl.DeviceIdType.MESH
 STRIP = 16
 LAG_ROWS = 224
-UNROLL = 16
+UNROLL = 32
 LOG2E = math.log2(math.e)
 OCTAVES = 22
 CODES = 65535.0 / OCTAVES

time: 28.6 us -> 28.1 us (0.983)
  Pallas kernels: 26.5 us -> 26 us
    pallas_call x1, Pallas kernels: 26.5 us -> 26 us  [shards(): pl.pallas_call(functools.partial(kernel, n, n_tx, n_ty, 2.0 / (samples *...]
where the time goes in v4:
time: 28.1 us; the launch traced here: 28 us
  Pallas kernels  26 us (93%)
  other arithmetic  1.92 us (7%)
    pallas_call x1, Pallas kernels, shards(): pl.pallas_call(functools.partial(kernel, n, n_tx, n_ty, 2.0 / (samples *...  26 us
    select_n x1, other arithmetic, decode(): return jnp.where(wide == -32768, 0.0, value)  1.92 us

profile of v4, /device:TPU:0, one launch (start us, length us, event | category | flops | bytes accessed | tf_op | source)
XLA Modules:
  0.0 28.0 jit_solution(15075878233596683155)
XLA Ops:
  0.0 26.0 %shard_map.64 = s16[4,256,128]{2,1,0:T(8,128)(2,1)} custom-call(bf16[32,256,128]{2,1,0:T(8,128)(2,1)} %vol.1, s32[1,256,128]{2,1,0:T(8,128)} %start_hbm.1, s32[1,256,128]{2,1,0:T(8,128)} %stop_hbm.1, s32[1,32]{1,0:T(1,128)} %bitcast.3, f32[2,4]{1,0:T(2,128)} %bitcast.2, s32[4]{0:T(128)} %order.1), custom_call_target="tpu_custom_call" | custom-call | tf_op jit(solution)/shard_map/pallas_call | solution.py:305
  26.0 1.9 %fusion.3 = f32[4,256,128]{2,1,0:T(8,128)} fusion(s16[4,256,128]{2,1,0:T(8,128)(2,1)} %shard_map.64), kind=kLoop, calls=%fused_computation.5 | loop fusion | flops 786432 | bytes 786432 | tf_op jit(solution)/shard_map/jit(_where)/select_n | solution.py:28
